TPU v7x, 32 devices: a whole 2x2x4 slice. The times are simulated.
32 devices in a mesh: gx: 4 (over x, core), gy: 8 (over z, y).
Axes of the slice: x: 2, y: 2, z: 4, core: 2. Of those that a mesh axis runs over, the one named last changes fastest.
Arguments:
- layer_input: bfloat16 [8192, 1152], P(('gx', 'gy')), may hold values from -6 to 6
- norm_one_gain: bfloat16 [1152], P('gy'), may hold values from 0.5 to 1.5
- norm_one_bias: bfloat16 [1152], P('gy'), may hold values from -1.75 to 1.75
- query_weight: bfloat16 [1152, 1152], P('gx', 'gy'), may hold values from -0.1875 to 0.1875
- query_bias: bfloat16 [1152], P('gy'), may hold values from -1.75 to 1.75
- key_weight: bfloat16 [1152, 1152], P('gx', 'gy'), may hold values from -0.1875 to 0.1875
- value_weight: bfloat16 [1152, 1152], P('gx', 'gy'), may hold values from -0.1875 to 0.1875
- value_bias: bfloat16 [1152], P('gy'), may hold values from -1.75 to 1.75
- output_weight: bfloat16 [1152, 1152], P('gy', 'gx'), may hold values from -1 to 1
- output_bias: bfloat16 [1152], P('gy'), may hold values from -1.75 to 1.75
- norm_two_gain: bfloat16 [1152], P('gy'), may hold values from 0.5 to 1.5
- norm_two_bias: bfloat16 [1152], P('gy'), may hold values from -1.75 to 1.75
- up_weight: bfloat16 [1152, 4304], P('gx', 'gy'), may hold values from -0.1875 to 0.1875
- up_bias: bfloat16 [4304], P('gy'), may hold values from -1.75 to 1.75
- down_weight: bfloat16 [4304, 1152], P('gy', 'gx'), may hold values from -0.09375 to 0.09375
- down_bias: bfloat16 [1152], P('gy'), may hold values from -1.75 to 1.75
- cotangent: bfloat16 [8192, 1152], P(('gx', 'gy')), may hold values from -6 to 6
Outputs:
- layer_output: bfloat16 [8192, 1152], P(('gx', 'gy'))
- grad_input: bfloat16 [8192, 1152], P(('gx', 'gy'))
- grad_norm_one_gain: float32 [1152], P('gy')
- grad_norm_one_bias: float32 [1152], P('gy')
- grad_query_weight: float32 [1152, 1152], P('gx', 'gy')
- grad_query_bias: float32 [1152], P('gy')
- grad_key_weight: float32 [1152, 1152], P('gx', 'gy')
- grad_value_weight: float32 [1152, 1152], P('gx', 'gy')
- grad_value_bias: float32 [1152], P('gy')
- grad_output_weight: float32 [1152, 1152], P('gy', 'gx')
- grad_output_bias: float32 [1152], P('gy')
- grad_norm_two_gain: float32 [1152], P('gy')
- grad_norm_two_bias: float32 [1152], P('gy')
- grad_up_weight: float32 [1152, 4304], P('gx', 'gy')
- grad_up_bias: float32 [4304], P('gy')
- grad_down_weight: float32 [4304, 1152], P('gy', 'gx')
- grad_down_bias: float32 [1152], P('gy')
All inputs are finite; a program needn't handle non-finite values.
Results may differ from a plain program's by a relative error of at most 0.023.
Values may be sent and summed in bfloat16 or wider, within the bound.
A program may use at most 192 MiB of HBM per device.

v0:
```python
import jax
import jax.numpy as jnp
from jax import lax
from jax.sharding import PartitionSpec as P

HD = 72
LENGTH = 1024


def dot_plain(left, right):
    return jnp.dot(left, right, preferred_element_type=jnp.float32)


def dot_right_t(left, right):
    return lax.dot_general(
        left, right, (((1,), (1,)), ((), ())), preferred_element_type=jnp.float32
    )


def dot_left_t(left, right):
    return lax.dot_general(
        left, right, (((0,), (0,)), ((), ())), preferred_element_type=jnp.float32
    )


def normalize(rows):
    center = rows - jnp.mean(rows, axis=-1, keepdims=True)
    inverse = lax.rsqrt(jnp.mean(center * center, axis=-1, keepdims=True) + 1e-06)
    return (center * inverse, inverse)


def gelu_tanh(value):
    return jax.nn.gelu(value, approximate=True)


def image_shape(array):
    heads = array.shape[1] // HD
    return (array.shape[0] // LENGTH, LENGTH, heads, HD)


def attend(query, key, value):
    shape = image_shape(query)
    scale = HD ** (-0.5)

    def one_image(carry, pieces):
        q_img, k_img, v_img = pieces
        scores = (
            jnp.einsum("qhd,khd->hqk", q_img, k_img, preferred_element_type=jnp.float32) * scale
        )
        top = jnp.max(scores, axis=-1, keepdims=True)
        expo = jnp.exp(scores - top)
        total = jnp.sum(expo, axis=-1, keepdims=True)
        probs = (expo / total).astype(jnp.bfloat16)
        mixed = jnp.einsum("hqk,khd->qhd", probs, v_img, preferred_element_type=jnp.float32).astype(
            jnp.bfloat16
        )
        return (carry, (mixed, (top + jnp.log(total))[..., 0]))

    _, (mixed, lse) = lax.scan(
        one_image, 0, (query.reshape(shape), key.reshape(shape), value.reshape(shape))
    )
    return (mixed.reshape(query.shape), lse)


def attend_back(query, key, value, lse, d_mixed):
    shape = image_shape(query)
    scale = HD ** (-0.5)

    def one_image(carry, pieces):
        q_img, k_img, v_img, lse_img, dm_img = pieces
        scores = (
            jnp.einsum("qhd,khd->hqk", q_img, k_img, preferred_element_type=jnp.float32) * scale
        )
        probs = jnp.exp(scores - lse_img[..., None])
        d_probs = jnp.einsum("qhd,khd->hqk", dm_img, v_img, preferred_element_type=jnp.float32)
        d_scores = (probs * (d_probs - jnp.sum(d_probs * probs, axis=-1, keepdims=True))).astype(
            jnp.bfloat16
        )
        d_value = jnp.einsum(
            "hqk,qhd->khd", probs.astype(jnp.bfloat16), dm_img, preferred_element_type=jnp.float32
        ).astype(jnp.bfloat16)
        d_query = (
            jnp.einsum("hqk,khd->qhd", d_scores, k_img, preferred_element_type=jnp.float32) * scale
        ).astype(jnp.bfloat16)
        d_key = (
            jnp.einsum("hqk,qhd->khd", d_scores, q_img, preferred_element_type=jnp.float32) * scale
        ).astype(jnp.bfloat16)
        return (carry, (d_query, d_key, d_value))

    _, (d_query, d_key, d_value) = lax.scan(
        one_image,
        0,
        (
            query.reshape(shape),
            key.reshape(shape),
            value.reshape(shape),
            lse,
            d_mixed.reshape(shape),
        ),
    )
    return (d_query.reshape(query.shape), d_key.reshape(query.shape), d_value.reshape(query.shape))


def forward_pass(
    complete,
    layer_input,
    norm_one_gain,
    norm_one_bias,
    query_weight,
    query_bias,
    key_weight,
    value_weight,
    value_bias,
    output_weight,
    output_bias,
    norm_two_gain,
    norm_two_bias,
    up_weight,
    up_bias,
    down_weight,
    down_bias,
):
    w_query, w_key, w_value, w_output, w_up, w_down = (
        lax.all_gather(query_weight, "gx", axis=0, tiled=True),
        lax.all_gather(key_weight, "gx", axis=0, tiled=True),
        lax.all_gather(value_weight, "gx", axis=0, tiled=True),
        lax.all_gather(output_weight, "gx", axis=1, tiled=True),
        lax.all_gather(up_weight, "gx", axis=0, tiled=True),
        lax.all_gather(down_weight, "gx", axis=1, tiled=True),
    )
    rows_one, gain_one, shift_one, out_shift, down_shift = (
        lax.all_gather(layer_input, "gy", axis=0, tiled=True),
        lax.all_gather(norm_one_gain, "gy", axis=0, tiled=True),
        lax.all_gather(norm_one_bias, "gy", axis=0, tiled=True),
        lax.all_gather(output_bias, "gy", axis=0, tiled=True),
        lax.all_gather(down_bias, "gy", axis=0, tiled=True),
    )
    hat_one, inv_one = normalize(rows_one.astype(jnp.float32))
    normed = (hat_one * gain_one.astype(jnp.float32) + shift_one.astype(jnp.float32)).astype(
        jnp.bfloat16
    )
    query = (dot_plain(normed, w_query) + query_bias.astype(jnp.float32)).astype(jnp.bfloat16)
    key = dot_plain(normed, w_key).astype(jnp.bfloat16)
    value = (dot_plain(normed, w_value) + value_bias.astype(jnp.float32)).astype(jnp.bfloat16)
    mixed, lse = attend(query, key, value)
    attn_part = lax.psum_scatter(
        dot_plain(mixed, w_output).astype(jnp.bfloat16), "gy", scatter_dimension=0, tiled=True
    ).astype(jnp.float32)
    residual = layer_input.astype(jnp.float32) + attn_part + out_shift.astype(jnp.float32)
    rows_two, gain_two, shift_two = (
        lax.all_gather(residual.astype(jnp.bfloat16), "gy", axis=0, tiled=True),
        lax.all_gather(norm_two_gain, "gy", axis=0, tiled=True),
        lax.all_gather(norm_two_bias, "gy", axis=0, tiled=True),
    )
    hat_two, inv_two = normalize(rows_two.astype(jnp.float32))
    normed_two = (hat_two * gain_two.astype(jnp.float32) + shift_two.astype(jnp.float32)).astype(
        jnp.bfloat16
    )
    upper = dot_plain(normed_two, w_up) + up_bias.astype(jnp.float32)
    active = gelu_tanh(upper).astype(jnp.bfloat16)
    result = residual
    if complete:
        mlp_part = lax.psum_scatter(
            dot_plain(active, w_down).astype(jnp.bfloat16), "gy", scatter_dimension=0, tiled=True
        ).astype(jnp.float32)
        result = residual + mlp_part + down_shift.astype(jnp.float32)
    return (
        w_query,
        w_key,
        w_value,
        w_output,
        w_up,
        w_down,
        hat_one,
        inv_one,
        normed,
        query,
        key,
        value,
        mixed,
        lse,
        hat_two,
        inv_two,
        normed_two,
        upper,
        active,
        result,
        gain_one,
        gain_two,
    )


def shards(
    layer_input,
    norm_one_gain,
    norm_one_bias,
    query_weight,
    query_bias,
    key_weight,
    value_weight,
    value_bias,
    output_weight,
    output_bias,
    norm_two_gain,
    norm_two_bias,
    up_weight,
    up_bias,
    down_weight,
    down_bias,
    cotangent,
):
    inputs = (
        layer_input,
        norm_one_gain,
        norm_one_bias,
        query_weight,
        query_bias,
        key_weight,
        value_weight,
        value_bias,
        output_weight,
        output_bias,
        norm_two_gain,
        norm_two_bias,
        up_weight,
        up_bias,
        down_weight,
        down_bias,
    )
    saved = forward_pass(True, *inputs)
    layer_output = saved[19].astype(jnp.bfloat16)
    again, layer_output = lax.optimization_barrier((inputs, layer_output))
    saved = forward_pass(False, *again)
    (
        w_query,
        w_key,
        w_value,
        w_output,
        w_up,
        w_down,
        hat_one,
        inv_one,
        normed,
        query,
        key,
        value,
        mixed,
        lse,
        hat_two,
        inv_two,
        normed_two,
        upper,
        active,
        result,
        gain_one,
        gain_two,
    ) = saved
    local = layer_input.shape[0]
    start = lax.axis_index("gy") * local
    grad_rows = lax.all_gather(cotangent, "gy", axis=0, tiled=True)
    d_active = dot_right_t(grad_rows, w_down)
    _, gelu_pull = jax.vjp(gelu_tanh, upper)
    d_upper = gelu_pull(d_active)[0].astype(jnp.bfloat16)
    grad_up_weight, grad_down_weight = (
        lax.psum_scatter(
            dot_left_t(normed_two, d_upper).astype(jnp.bfloat16),
            "gx",
            scatter_dimension=0,
            tiled=True,
        ).astype(jnp.float32),
        lax.psum_scatter(
            dot_left_t(active, grad_rows).astype(jnp.bfloat16),
            "gx",
            scatter_dimension=1,
            tiled=True,
        ).astype(jnp.float32),
    )
    d_normed_two = lax.psum_scatter(
        dot_right_t(d_upper, w_up).astype(jnp.bfloat16), "gy", scatter_dimension=0, tiled=True
    ).astype(jnp.float32)
    hat_two_local = lax.dynamic_slice_in_dim(hat_two, start, local, 0)
    inv_two_local = lax.dynamic_slice_in_dim(inv_two, start, local, 0)
    scaled_two = d_normed_two * gain_two.astype(jnp.float32)
    mean_two = jnp.mean(scaled_two, axis=-1, keepdims=True)
    proj_two = jnp.mean(scaled_two * hat_two_local, axis=-1, keepdims=True)
    cot_float = cotangent.astype(jnp.float32)
    d_residual = cot_float + inv_two_local * (scaled_two - mean_two - hat_two_local * proj_two)
    part_two_gain = jnp.sum(d_normed_two * hat_two_local, axis=0)
    part_two_bias = jnp.sum(d_normed_two, axis=0)
    part_up_bias = jnp.sum(d_upper.astype(jnp.float32), axis=0)
    part_down_bias = jnp.sum(cot_float, axis=0)
    grad_attn = lax.all_gather(d_residual.astype(jnp.bfloat16), "gy", axis=0, tiled=True)
    part_output_bias = jnp.sum(d_residual, axis=0)
    d_mixed = dot_right_t(grad_attn, w_output).astype(jnp.bfloat16)
    d_query, d_key, d_value = attend_back(query, key, value, lse, d_mixed)
    grad_query_weight, grad_key_weight, grad_value_weight, grad_output_weight = (
        lax.psum_scatter(
            dot_left_t(normed, d_query).astype(jnp.bfloat16), "gx", scatter_dimension=0, tiled=True
        ).astype(jnp.float32),
        lax.psum_scatter(
            dot_left_t(normed, d_key).astype(jnp.bfloat16), "gx", scatter_dimension=0, tiled=True
        ).astype(jnp.float32),
        lax.psum_scatter(
            dot_left_t(normed, d_value).astype(jnp.bfloat16), "gx", scatter_dimension=0, tiled=True
        ).astype(jnp.float32),
        lax.psum_scatter(
            dot_left_t(mixed, grad_attn).astype(jnp.bfloat16), "gx", scatter_dimension=1, tiled=True
        ).astype(jnp.float32),
    )
    d_normed = lax.psum_scatter(
        (
            dot_right_t(d_query, w_query)
            + dot_right_t(d_key, w_key)
            + dot_right_t(d_value, w_value)
        ).astype(jnp.bfloat16),
        "gy",
        scatter_dimension=0,
        tiled=True,
    ).astype(jnp.float32)
    hat_one_local = lax.dynamic_slice_in_dim(hat_one, start, local, 0)
    inv_one_local = lax.dynamic_slice_in_dim(inv_one, start, local, 0)
    scaled_one = d_normed * gain_one.astype(jnp.float32)
    mean_one = jnp.mean(scaled_one, axis=-1, keepdims=True)
    proj_one = jnp.mean(scaled_one * hat_one_local, axis=-1, keepdims=True)
    grad_input = (
        d_residual + inv_one_local * (scaled_one - mean_one - hat_one_local * proj_one)
    ).astype(jnp.bfloat16)
    part_one_gain = jnp.sum(d_normed * hat_one_local, axis=0)
    part_one_bias = jnp.sum(d_normed, axis=0)
    part_query_bias = jnp.sum(d_query.astype(jnp.float32), axis=0)
    part_value_bias = jnp.sum(d_value.astype(jnp.float32), axis=0)
    feat_one_gain, feat_one_bias, feat_output_bias, feat_two_gain, feat_two_bias, feat_down_bias = (
        lax.psum_scatter(part_one_gain, "gy", scatter_dimension=0, tiled=True),
        lax.psum_scatter(part_one_bias, "gy", scatter_dimension=0, tiled=True),
        lax.psum_scatter(part_output_bias, "gy", scatter_dimension=0, tiled=True),
        lax.psum_scatter(part_two_gain, "gy", scatter_dimension=0, tiled=True),
        lax.psum_scatter(part_two_bias, "gy", scatter_dimension=0, tiled=True),
        lax.psum_scatter(part_down_bias, "gy", scatter_dimension=0, tiled=True),
    )
    (
        grad_one_gain,
        grad_one_bias,
        grad_query_bias,
        grad_value_bias,
        grad_output_bias,
        grad_two_gain,
        grad_two_bias,
        grad_up_bias,
        grad_down_bias,
    ) = lax.psum(
        (
            feat_one_gain,
            feat_one_bias,
            part_query_bias,
            part_value_bias,
            feat_output_bias,
            feat_two_gain,
            feat_two_bias,
            part_up_bias,
            feat_down_bias,
        ),
        "gx",
    )
    return (
        layer_output,
        grad_input,
        grad_one_gain,
        grad_one_bias,
        grad_query_weight,
        grad_query_bias,
        grad_key_weight,
        grad_value_weight,
        grad_value_bias,
        grad_output_weight,
        grad_output_bias,
        grad_two_gain,
        grad_two_bias,
        grad_up_weight,
        grad_up_bias,
        grad_down_weight,
        grad_down_bias,
    )


def solution(mesh):
    return jax.shard_map(
        shards,
        mesh=mesh,
        in_specs=(
            P(("gx", "gy"), None),
            P("gy"),
            P("gy"),
            P("gx", "gy"),
            P("gy"),
            P("gx", "gy"),
            P("gx", "gy"),
            P("gy"),
            P("gy", "gx"),
            P("gy"),
            P("gy"),
            P("gy"),
            P("gx", "gy"),
            P("gy"),
            P("gy", "gx"),
            P("gy"),
            P(("gx", "gy"), None),
        ),
        out_specs=(
            P(("gx", "gy"), None),
            P(("gx", "gy"), None),
            P("gy"),
            P("gy"),
            P("gx", "gy"),
            P("gy"),
            P("gx", "gy"),
            P("gx", "gy"),
            P("gy"),
            P("gy", "gx"),
            P("gy"),
            P("gy"),
            P("gy"),
            P("gx", "gy"),
            P("gy"),
            P("gy", "gx"),
            P("gy"),
        ),
        check_vma=False,
    )
```

profile of v0, /device:TPU:0, one launch (start us, length us, event | category | flops | bytes accessed | tf_op | source)
XLA Modules:
  0.0 1392.4 jit_solution(10019122874200687494)
XLA Ops:
  16.4 39.7 %all-reduce.20 = (bf16[1152]{0:T(1024)(128)(2,1)S(1)}, bf16[1152]{0:T(1024)(128)(2,1)S(1)}, bf16[1152]{0:T(1024)(128)(2,1)S(1)}, bf16[1152]{0:T(1024)(128)(2,1)S...) all-reduce(bf16[1152]{0:T(1024)(128)(2,1)S(1)} %dynamic-update-slic, ...), channel_id=1, replica_groups=mesh['gx'=4,'gy'=8] {'gy'}, use_global_device_ids=true, to_apply=%add.1 | all-reduce | flops 6912 | bytes 27648
  114.2 18.5 %while.36 = (s32[]{:T(128)}, bf16[2,1024,2,72]{1,3,2,0:T(8,128)(2,1)S(1)}, bf16[2,1024,2,72]{1,3,2,0:T(8,128)(2,1)S(1)}, bf16[2,1024,2,72]{1,3,2,0:T(8,128)(2,1)...) while((s32[]{:T(128)}, bf16[2,1024,2,72]{1,3,2,0:T(8,128)(2,1)S(1)}, ...), condition=%wide.region_5.6_spmd, body=%wide.region_2.5_spmd.sunk | while | flops 614614016 | bytes 17975372 | solution.py:59
  137.3 93.5 %reduce-scatter.20.cloned.1.call-done = bf16[256,1152]{1,0:T(8,128)(2,1)} async-done(((bf16[2048,1152]{1,0:T(8,128)(2,1)}), bf16[256,1152]{1,0:T(8,128)(2,1)}) %reduce-scatter.20.cloned.1.call-update) | async-done | bytes 589840 | tf_op jit(solution)/shard_map/reduce_scatter | solution.py:146
  234.3 78.9 %all-gather.21.cloned.1.call-done = bf16[2048,1152]{1,0:T(8,128)(2,1)} async-done(((bf16[256,1152]{1,0:T(8,128)(2,1)}), bf16[2048,1152]{1,0:T(8,128)(2,1)}) %all-gather.21.cloned.1.call-update) | async-done | bytes 4718608 | tf_op jit(solution)/shard_map/all_gather | solution.py:151
  318.4 13.5 all-gather.23.cloned.1.call-done
  331.9 20.6 %all-gather.25.cloned.1.call-done = bf16[538,1152]{0,1:T(8,128)(2,1)} async-done(((bf16[538,288]{0,1:T(8,128)(2,1)}), bf16[538,1152]{0,1:T(8,128)(2,1)}) %all-gather.25.cloned.1.call-update) | async-done | bytes 1239568 | tf_op jit(solution)/shard_map/all_gather | solution.py:129
  352.4 12.9 convolution_convert_fusion.2
  365.6 95.5 %reduce-scatter.22.cloned.1.call-done = bf16[256,1152]{1,0:T(8,128)(2,1)} async-done(((bf16[2048,1152]{1,0:T(8,128)(2,1)}), bf16[256,1152]{1,0:T(8,128)(2,1)}) %reduce-scatter.22.cloned.1.call-update) | async-done | bytes 589840 | tf_op jit(solution)/shard_map/reduce_scatter | solution.py:163
  464.6 37.2 %all-reduce.19 = (bf16[1152]{0:T(1024)(128)(2,1)}, bf16[1152]{0:T(1024)(128)(2,1)}, bf16[1152]{0:T(1024)(128)(2,1)S(1)}, bf16[1152]{0:T(1024)(128)(2,1)S(1)}, bf16[1152]{0:T(1024)(128)(2,1)}) all-reduce(bf16[1152]{0:T(1024)(128)(2,1)S(1)} %dynamic-update-slice.10, ...), channel_id=1, replica_groups=mesh['gx'=4,'gy'=8] {'gy'}, use_global_device_ids=true, to_apply=%add.10 | all-reduce | flops 5760 | bytes 23040
  532.1 11.5 all-gather.27.cloned.1.call-done
  582.5 92.9 %reduce-scatter.24.cloned.1.call-done = bf16[256,1152]{1,0:T(8,128)(2,1)} async-done(((bf16[2048,1152]{1,0:T(8,128)(2,1)}), bf16[256,1152]{1,0:T(8,128)(2,1)}) %reduce-scatter.24.cloned.1.call-update) | async-done | bytes 589840 | tf_op jit(solution)/shard_map/reduce_scatter | solution.py:146
  679.5 78.4 %all-gather.29.cloned.1.call-done = bf16[2048,1152]{1,0:T(8,128)(2,1)} async-done(((bf16[256,1152]{1,0:T(8,128)(2,1)}), bf16[2048,1152]{1,0:T(8,128)(2,1)}) %all-gather.29.cloned.1.call-update) | async-done | bytes 4718608 | tf_op jit(solution)/shard_map/all_gather | solution.py:151
  763.1 13.5 all-gather.35.cloned.1.call-done
  785.0 73.7 %all-gather.33.cloned.1.call-done = bf16[2048,1152]{1,0:T(8,128)(2,1)} async-done(((bf16[256,1152]{1,0:T(8,128)(2,1)}), bf16[2048,1152]{1,0:T(8,128)(2,1)}) %all-gather.33.cloned.1.call-update) | async-done | bytes 4718608 | tf_op jit(solution)/shard_map/all_gather | solution.py:260
  858.7 18.7 %all-gather.31.cloned.1.call-done = bf16[538,1152]{0,1:T(8,128)(2,1)} async-done(((bf16[538,288]{0,1:T(8,128)(2,1)}), bf16[538,1152]{0,1:T(8,128)(2,1)}) %all-gather.31.cloned.1.call-update) | async-done | bytes 1239568 | tf_op jit(solution)/shard_map/all_gather | solution.py:129
  903.5 88.8 %reduce-scatter.26.cloned.1.call-done = bf16[256,1152]{1,0:T(8,128)(2,1)} async-done(((bf16[2048,1152]{1,0:T(8,128)(2,1)}), bf16[256,1152]{1,0:T(8,128)(2,1)}) %reduce-scatter.26.cloned.1.call-update) | async-done | bytes 589840 | tf_op jit(solution)/shard_map/reduce_scatter | solution.py:278
  1016.9 61.1 %all-gather.37.cloned.1.call-done = bf16[2048,1152]{1,0:T(8,128)(2,1)} async-done(((bf16[256,1152]{1,0:T(8,128)(2,1)}), bf16[2048,1152]{1,0:T(8,128)(2,1)}) %all-gather.37.cloned.1.call-update) | async-done | bytes 4718608 | tf_op jit(solution)/shard_map/all_gather | solution.py:292
  1095.1 21.3 %while.38 = (s32[]{:T(128)}, bf16[2,1024,2,72]{1,3,2,0:T(8,128)(2,1)}, bf16[2,1024,2,72]{1,3,2,0:T(8,128)(2,1)}, bf16[2,1024,2,72]{1,3,2,0:T(8,128)(2,1)S(1)}, b...) while((s32[]{:T(128)}, ...), condition=%wide.region_24.25_spmd, body=%wide.region_22.24_spmd.sunk | while | flops 1535850496 | bytes 77722880 | solution.py:90
  1162.5 22.7 %reduce-scatter.34.cloned.1.call-done = bf16[288,144]{1,0:T(8,128)(2,1)} async-done(((bf16[1152,144]{1,0:T(8,128)(2,1)}), bf16[288,144]{1,0:T(8,128)(2,1)}) %reduce-scatter.34.cloned.1.call-update) | async-done | bytes 82960
  1187.0 22.9 %reduce-scatter.36.cloned.1.call-done = bf16[288,144]{1,0:T(8,128)(2,1)} async-done(((bf16[1152,144]{1,0:T(8,128)(2,1)}), bf16[288,144]{1,0:T(8,128)(2,1)}) %reduce-scatter.36.cloned.1.call-update) | async-done | bytes 82960
  1211.6 22.7 %reduce-scatter.38.cloned.1.call-done = bf16[288,144]{1,0:T(8,128)(2,1)} async-done(((bf16[1152,144]{1,0:T(8,128)(2,1)}), bf16[288,144]{1,0:T(8,128)(2,1)}) %reduce-scatter.38.cloned.1.call-update) | async-done | bytes 82960
  1236.0 97.2 %reduce-scatter.28.cloned.1.call-done = bf16[256,1152]{1,0:T(8,128)(2,1)} async-done(((bf16[2048,1152]{1,0:T(8,128)(2,1)}), bf16[256,1152]{1,0:T(8,128)(2,1)}) %reduce-scatter.28.cloned.1.call-update) | async-done | bytes 589840 | tf_op jit(solution)/shard_map/reduce_scatter | solution.py:310
  1335.2 36.4 %all-reduce.17 = (f32[1152]{0:T(1024)S(1)}, f32[1152]{0:T(1024)S(1)}, f32[1152]{0:T(1024)S(1)}, f32[1152]{0:T(1024)S(1)}, f32[1152]{0:T(1024)S(1)}, /*index=5*/f32[1152]{0:T(1024)S(1)}) all-reduce(f32[1152]{0:T(1024)S(1)} %get-tuple-element.226, f32[1152]{0:T(1024)S(1)} %get-tuple-element.231, ...), channel_id=7, replica_groups=mesh['gx'=4,'gy'=8] {'gy'}, use_global_device_ids=true, to_apply=%region_29.30.clone | all-reduce | flops 6912 | bytes 55296
  1372.1 10.7 all-reduce.18
  (368 shorter events, 341.3 us)
Async XLA Ops:
  7.2 86.2 %all-gather.19.cloned.1.call-start = ((), (), s32[]{:S(2)}) async-start(), calls=%async_computation.11 | async-start | bytes 5308416 | tf_op jit(solution)/shard_map/all_gather | solution.py:132
  7.9 222.8 %reduce-scatter.20.cloned.1.call-start = ((), (), s32[]{:S(2)}) async-start(), calls=%async_computation.12 | async-start | bytes 5308416 | tf_op jit(solution)/shard_map/reduce_scatter | solution.py:146
  137.2 176.0 %all-gather.21.cloned.1.call-start = ((), (), s32[]{:S(2)}) async-start(), calls=%async_computation.13 | async-start | bytes 5308416 | tf_op jit(solution)/shard_map/all_gather | solution.py:151
  232.9 99.0 %all-gather.23.cloned.1.call-start = ((), (), s32[]{:S(2)}) async-start(), calls=%async_computation.14 | async-start | bytes 1843200 | tf_op jit(solution)/shard_map/all_gather | solution.py:128
  233.4 119.0 %all-gather.25.cloned.1.call-start = ((), (), s32[]{:S(2)}) async-start(), calls=%async_computation.15 | async-start | bytes 1843200 | tf_op jit(solution)/shard_map/all_gather | solution.py:129
  234.0 227.0 %reduce-scatter.22.cloned.1.call-start = ((), (), s32[]{:S(2)}) async-start(), calls=%async_computation.16 | async-start | bytes 5308416 | tf_op jit(solution)/shard_map/reduce_scatter | solution.py:163
  365.5 178.0 %all-gather.27.cloned.1.call-start = ((), (), s32[]{:S(2)}) async-start(), calls=%async_computation.17 | async-start | bytes 5308416 | tf_op jit(solution)/shard_map/all_gather | solution.py:132
  463.2 212.2 %reduce-scatter.24.cloned.1.call-start = ((), (), s32[]{:S(2)}) async-start(), calls=%async_computation.18 | async-start | bytes 5308416 | tf_op jit(solution)/shard_map/reduce_scatter | solution.py:146
  581.9 176.0 %all-gather.29.cloned.1.call-start = ((), (), s32[]{:S(2)}) async-start(), calls=%async_computation.19 | async-start | bytes 5308416 | tf_op jit(solution)/shard_map/all_gather | solution.py:151
  677.5 99.0 %all-gather.35.cloned.1.call-start = ((), (), s32[]{:S(2)}) async-start(), calls=%async_computation.22 | async-start | bytes 1843200 | tf_op jit(solution)/shard_map/all_gather | solution.py:128
  678.1 180.6 %all-gather.33.cloned.1.call-start = ((), (), s32[]{:S(2)}) async-start(), calls=%async_computation.21 | async-start | bytes 5308416 | tf_op jit(solution)/shard_map/all_gather | solution.py:260
  678.9 198.5 %all-gather.31.cloned.1.call-start = ((), (), s32[]{:S(2)}) async-start(), calls=%async_computation.20 | async-start | bytes 1843200 | tf_op jit(solution)/shard_map/all_gather | solution.py:129
  679.0 198.4 %copy-start.48 = (f32[538]{0:T(1024)}, f32[538]{0:T(1024)S(1)}, u32[]{:S(2)}) copy-start(f32[538]{0:T(1024)S(1)} %convert_element_type.293) | copy-start | bytes 6460
  679.0 313.3 %copy-start.29 = (f32[1152]{0:T(1024)}, f32[1152]{0:T(1024)S(1)}, u32[]{:S(2)}) copy-start(f32[1152]{0:T(1024)S(1)} %convert_element_type.290) | copy-start | bytes 13828
  679.4 312.9 %reduce-scatter.26.cloned.1.call-start = ((), (), s32[]{:S(2)}) async-start(), calls=%async_computation.23 | async-start | bytes 5308416 | tf_op jit(solution)/shard_map/reduce_scatter | solution.py:278
  896.9 181.1 %all-gather.37.cloned.1.call-start = ((), (), s32[]{:S(2)}) async-start(), calls=%async_computation.24 | async-start | bytes 5308416 | tf_op jit(solution)/shard_map/all_gather | solution.py:292
  998.3 156.1 %reduce-scatter.32.cloned.1.call-start = ((), (), s32[]{:S(2)}) async-start(), calls=%async_computation.27 | async-start | bytes 1843200 | tf_op jit(solution)/shard_map/reduce_scatter | solution.py:271
  1007.4 148.9 %reduce-scatter.30.cloned.1.call-start = ((), (), s32[]{:S(2)}) async-start(), calls=%async_computation.26 | async-start | bytes 1843200 | tf_op jit(solution)/shard_map/reduce_scatter | solution.py:265
  1016.9 143.9 %reduce-scatter.40.cloned.1.call-start = ((), (), s32[]{:S(2)}) async-start(), calls=%async_computation.31 | async-start | bytes 737280
  1093.1 92.1 %reduce-scatter.34.cloned.1.call-start = ((), (), s32[]{:S(2)}) async-start(), calls=%async_computation.28 | async-start | bytes 737280
  1122.7 87.1 %reduce-scatter.36.cloned.1.call-start = ((), (), s32[]{:S(2)}) async-start(), calls=%async_computation.29 | async-start | bytes 737280
  1130.6 103.7 %reduce-scatter.38.cloned.1.call-start = ((), (), s32[]{:S(2)}) async-start(), calls=%async_computation.30 | async-start | bytes 737280
  1143.2 190.0 %reduce-scatter.28.cloned.1.call-start = ((), (), s32[]{:S(2)}) async-start(), calls=%async_computation.25 | async-start | bytes 5308416 | tf_op jit(solution)/shard_map/reduce_scatter | solution.py:310
  1152.9 219.2 %copy-start.44 = (f32[538]{0:T(1024)S(1)}, f32[538]{0:T(1024)}, u32[]{:S(2)}) copy-start(f32[538]{0:T(1024)} %get-tuple-element.311) | copy-start | bytes 6460
  (59 other events, 3503.2 us)
Sparse Core Ops, SparseCore 0:
  10.2 83.0 all-gather.18
  137.4 93.3 reduce-scatter.19
  233.5 79.6 all-gather.20
  314.6 17.2 all-gather.22
  333.3 19.1 all-gather.24
  365.6 95.3 reduce-scatter.21
  463.4 80.1 all-gather.26
  582.0 93.3 reduce-scatter.23
  678.2 79.6 all-gather.28
  759.3 17.2 all-gather.34
  778.8 79.8 all-gather.32
  860.1 17.2 all-gather.30
  897.0 95.2 reduce-scatter.25
  998.3 79.6 all-gather.36
  1080.4 25.6 reduce-scatter.31
  1108.8 27.5 reduce-scatter.29
  1138.7 22.0 reduce-scatter.39
  1163.2 22.0 reduce-scatter.33
  1187.7 22.0 reduce-scatter.35
  1212.2 22.0 reduce-scatter.37
  1238.0 95.2 reduce-scatter.27
where the time goes:
time: 1400 us; the launch traced here: 1390 us
  waiting for transfers between devices  920 us (66%)
  blocking collectives  179 us (13%)
  matrix products  161 us (12%)
  other arithmetic  63.7 us (5%)
  local copies, waits for them, and re-layouts  50.3 us (4%)
  between operations  17 us (1%)
    reduce_scatter x2, waiting for transfers between devices, forward_pass(): lax.psum_scatter(dot_plain(mixed, w_output).astype(jnp.bfloat16), 'gy', s...  186 us
    all_gather x2, waiting for transfers between devices, forward_pass(): lax.all_gather(residual.astype(jnp.bfloat16), 'gy', axis=0, tiled=True)  157 us
    unnamed x3, blocking collectives  113 us
    reduce_scatter x1, waiting for transfers between devices, shards(): lax.psum_scatter((dot_right_t(d_query, w_query) + dot_right_t(d_key, w_ke...  97.2 us
    reduce_scatter x1, waiting for transfers between devices, forward_pass(): lax.psum_scatter(dot_plain(active, w_down).astype(jnp.bfloat16), 'gy', sc...  95.5 us
    reduce_scatter x1, waiting for transfers between devices, shards(): lax.psum_scatter(dot_right_t(d_upper, w_up).astype(jnp.bfloat16), 'gy', s...  88.8 us
    unnamed x25, waiting for transfers between devices  74 us
    all_gather x1, waiting for transfers between devices, shards(): grad_rows = lax.all_gather(cotangent, 'gy', axis=0, tiled=True)  73.7 us
  transfers between devices with their start and end apart: 21, of which 19 were waited for; matrix products, arithmetic and copies ran while one was open for 10% of the time, Pallas kernels for 0%

commit v1 on v0

--- a/solution.py
+++ b/solution.py
@@ -5,6 +5,27 @@
 
 HD = 72
 LENGTH = 1024
+
+
+def collect(shard, axis, dim):
+    size, here, rows = (lax.axis_size(axis), lax.axis_index(axis), shard.shape[dim])
+    right = [(i, (i + 1) % size) for i in range(size)]
+    backward = [(i, (i - 1) % size) for i in range(size)]
+    filled = jnp.zeros((*shard.shape[:dim], size * rows, *shard.shape[dim + 1 :]), shard.dtype)
+    filled = lax.dynamic_update_slice_in_dim(filled, shard, here * rows, axis=dim)
+    from_left = from_right = shard
+    middle = size // 2
+    for step in range(1, middle + 1):
+        from_left = lax.ppermute(from_left, axis, right)
+        filled = lax.dynamic_update_slice_in_dim(
+            filled, from_left, (here - step) % size * rows, axis=dim
+        )
+        if step < size - middle:
+            from_right = lax.ppermute(from_right, axis, backward)
+            filled = lax.dynamic_update_slice_in_dim(
+                filled, from_right, (here + step) % size * rows, axis=dim
+            )
+    return filled
 
 
 def dot_plain(left, right):
@@ -148,7 +169,7 @@
     ).astype(jnp.float32)
     residual = layer_input.astype(jnp.float32) + attn_part + out_shift.astype(jnp.float32)
     rows_two, gain_two, shift_two = (
-        lax.all_gather(residual.astype(jnp.bfloat16), "gy", axis=0, tiled=True),
+        collect(residual.astype(jnp.bfloat16), "gy", 0),
         lax.all_gather(norm_two_gain, "gy", axis=0, tiled=True),
         lax.all_gather(norm_two_bias, "gy", axis=0, tiled=True),
     )

time: 1400 us -> 1330 us (0.950)
  waiting for transfers between devices: 920 us -> 796 us
  starting transfers between devices: 1.86 us -> 35.4 us
  local copies, waits for them, and re-layouts: 50.3 us -> 64.3 us
    all_gather x2 -> x0, waiting for transfers between devices: 157 us -> none  [forward_pass(): lax.all_gather(residual.astype(jnp.bfloat16), 'gy', axis=0, tiled=True)]
    ppermute x0 -> x14, waiting for transfers between devices: none -> 138 us  [the longest x8 138 us: collect(): from_left = lax.ppermute(from_left, axis, right)]
    all_gather x1, waiting for transfers between devices: 73.7 us -> 0.01 us  [shards(): grad_rows = lax.all_gather(cotangent, 'gy', axis=0, tiled=True)]
    all_gather x2, waiting for transfers between devices: 39.2 us -> 0.02 us  [forward_pass(): lax.all_gather(down_weight, 'gx', axis=1, tiled=True)]
    reduce_scatter x2, waiting for transfers between devices: 186 us -> 222 us  [forward_pass(): lax.psum_scatter(dot_plain(mixed, w_output).astype(jnp.bfloat16), 'gy', s...]
    ppermute x0 -> x14, starting transfers between devices: none -> 34.1 us  [the longest x8 18.1 us: collect(): from_left = lax.ppermute(from_left, axis, right)]
    all_gather x2, waiting for transfers between devices: 27 us -> 0.05 us  [forward_pass(): lax.all_gather(up_weight, 'gx', axis=0, tiled=True)]
    unnamed x154 -> x158, local copies, waits for them, and re-layouts: 32.1 us -> 28.5 us
  transfers between devices with their start and end apart: 21 -> 33, of which waited for: 19 -> 20; matrix products, arithmetic and copies ran while one was open for 10% -> 13% of each run, Pallas kernels for 0% -> 0%
where the time goes in v1:
time: 1330 us
  waiting for transfers between devices  796 us (60%)
  blocking collectives  179 us (13%)
  matrix products  160 us (12%)
  other arithmetic  73.6 us (6%)
  local copies, waits for them, and re-layouts  64.3 us (5%)
  starting transfers between devices  35.4 us (3%)
  between operations  18.7 us (1%)
    reduce_scatter x2, waiting for transfers between devices, forward_pass(): lax.psum_scatter(dot_plain(mixed, w_output).astype(jnp.bfloat16), 'gy', s...  222 us
    ppermute x8, waiting for transfers between devices, collect(): from_left = lax.ppermute(from_left, axis, right)  138 us
    unnamed x3, blocking collectives  114 us
    reduce_scatter x1, waiting for transfers between devices, shards(): lax.psum_scatter((dot_right_t(d_query, w_query) + dot_right_t(d_key, w_ke...  97.1 us
    reduce_scatter x1, waiting for transfers between devices, forward_pass(): lax.psum_scatter(dot_plain(active, w_down).astype(jnp.bfloat16), 'gy', sc...  95.1 us
    reduce_scatter x1, waiting for transfers between devices, shards(): lax.psum_scatter(dot_right_t(d_upper, w_up).astype(jnp.bfloat16), 'gy', s...  87.1 us
    unnamed x23, waiting for transfers between devices  76.1 us
    all_gather x1, waiting for transfers between devices, shards(): lax.all_gather(d_residual.astype(jnp.bfloat16), 'gy', axis=0, tiled=True)  61 us
  transfers between devices with their start and end apart: 33, of which 20 were waited for; matrix products, arithmetic and copies ran while one was open for 13% of the time, Pallas kernels for 0%

profile of v1, /device:TPU:0, one launch (start us, length us, event | category | flops | bytes accessed | tf_op | source)
XLA Modules:
  0.0 1327.3 jit_solution(17789943679727513312)
XLA Ops:
  15.9 40.3 %all-reduce.20 = (bf16[1152]{0:T(1024)(128)(2,1)S(1)}, bf16[1152]{0:T(1024)(128)(2,1)S(1)}, bf16[1152]{0:T(1024)(128)(2,1)S(1)}, bf16[1152]{0:T(1024)(128)(2,1)}...) all-reduce(bf16[1152]{0:T(1024)(128)(2,1)S(1)} %dynamic-update-slice.1, ...), channel_id=1, replica_groups=mesh['gx'=4,'gy'=8] {'gy'}, use_global_device_ids=true, to_apply=%add.1 | all-reduce | flops 6912 | bytes 27648
  115.0 18.6 %while.36 = (s32[]{:T(128)}, bf16[2,1024,2,72]{1,3,2,0:T(8,128)(2,1)S(1)}, bf16[2,1024,2,72]{1,3,2,0:T(8,128)(2,1)S(1)}, bf16[2,1024,2,72]{1,3,2,0:T(8,128)(2,1)...) while((s32[]{:T(128)}, bf16[2,1024,2,72]{1,3,2,0:T(8,128)(2,1)S(1)}, ...), condition=%wide.region_5.6_spmd, body=%wide.region_2.5_spmd.sunk | while | flops 614614016 | bytes 17975364 | solution.py:80
  138.9 92.9 %reduce-scatter.20.cloned.1.call-done = bf16[256,1152]{1,0:T(8,128)(2,1)} async-done(((bf16[2048,1152]{1,0:T(8,128)(2,1)}), bf16[256,1152]{1,0:T(8,128)(2,1)}) %reduce-scatter.20.cloned.1.call-update) | async-done | bytes 589840 | tf_op jit(solution)/shard_map/reduce_scatter | solution.py:167
  240.0 22.0 %collective-permute-done = bf16[256,1152]{1,0:T(8,128)(2,1)S(1)} collective-permute-done((bf16[256,1152]{1,0:T(8,128)(2,1)S(1)}, bf16[256,1152]{1,0:T(8,128)(2,1)S(1)}, u32[]{:S(2)}, u32[]{:S(2)}) %collective-permute-start) | collective-permute-done | bytes 589856 | tf_op jit(solution)/shard_map/ppermute | solution.py:19
  270.1 18.7 %collective-permute-done.2 = bf16[256,1152]{1,0:T(8,128)(2,1)S(1)} collective-permute-done((bf16[256,1152]{1,0:T(8,128)(2,1)S(1)}, bf16[256,1152]{1,0:T(8,128)(2,1)S(1)}, u32[]{:S(2)}, u32[]{:S(2)}) %collective-permute-start.2) | collective-permute-done | bytes 589856 | tf_op jit(solution)/shard_map/ppermute | solution.py:19
  296.2 18.7 %collective-permute-done.4 = bf16[256,1152]{1,0:T(8,128)(2,1)S(1)} collective-permute-done((bf16[256,1152]{1,0:T(8,128)(2,1)S(1)}, bf16[256,1152]{1,0:T(8,128)(2,1)S(1)}, u32[]{:S(2)}, u32[]{:S(2)}) %collective-permute-start.4) | collective-permute-done | bytes 589856 | tf_op jit(solution)/shard_map/ppermute | solution.py:19
  338.6 13.0 convolution_convert_fusion.2
  351.7 95.1 %reduce-scatter.22.cloned.1.call-done = bf16[256,1152]{1,0:T(8,128)(2,1)} async-done(((bf16[2048,1152]{1,0:T(8,128)(2,1)}), bf16[256,1152]{1,0:T(8,128)(2,1)}) %reduce-scatter.22.cloned.1.call-update) | async-done | bytes 589840 | tf_op jit(solution)/shard_map/reduce_scatter | solution.py:184
  450.4 37.2 %all-reduce.19 = (bf16[1152]{0:T(1024)(128)(2,1)}, bf16[1152]{0:T(1024)(128)(2,1)}, bf16[1152]{0:T(1024)(128)(2,1)S(1)}, bf16[1152]{0:T(1024)(128)(2,1)S(1)}, bf16[1152]{0:T(1024)(128)(2,1)}) all-reduce(bf16[1152]{0:T(1024)(128)(2,1)S(1)} %dynamic-update-slice.10, ...), channel_id=1, replica_groups=mesh['gx'=4,'gy'=8] {'gy'}, use_global_device_ids=true, to_apply=%add.10 | all-reduce | flops 5760 | bytes 23040
  517.6 11.7 all-gather.23.cloned.1.call-done
  569.3 129.3 %reduce-scatter.24.cloned.1.call-done = bf16[256,1152]{1,0:T(8,128)(2,1)} async-done(((bf16[2048,1152]{1,0:T(8,128)(2,1)}), bf16[256,1152]{1,0:T(8,128)(2,1)}) %reduce-scatter.24.cloned.1.call-update) | async-done | bytes 589840 | tf_op jit(solution)/shard_map/reduce_scatter | solution.py:167
  706.8 21.6 %collective-permute-done.7 = bf16[256,1152]{1,0:T(8,128)(2,1)S(1)} collective-permute-done((bf16[256,1152]{1,0:T(8,128)(2,1)S(1)}, bf16[256,1152]{1,0:T(8,128)(2,1)S(1)}, u32[]{:S(2)}, u32[]{:S(2)}) %collective-permute-start.7) | collective-permute-done | bytes 589856 | tf_op jit(solution)/shard_map/ppermute | solution.py:19
  737.1 17.9 %collective-permute-done.9 = bf16[256,1152]{1,0:T(8,128)(2,1)S(1)} collective-permute-done((bf16[256,1152]{1,0:T(8,128)(2,1)S(1)}, bf16[256,1152]{1,0:T(8,128)(2,1)S(1)}, u32[]{:S(2)}, u32[]{:S(2)}) %collective-permute-start.9) | collective-permute-done | bytes 589856 | tf_op jit(solution)/shard_map/ppermute | solution.py:19
  763.8 17.3 %collective-permute-done.11 = bf16[256,1152]{1,0:T(8,128)(2,1)S(1)} collective-permute-done((bf16[256,1152]{1,0:T(8,128)(2,1)S(1)}, bf16[256,1152]{1,0:T(8,128)(2,1)S(1)}, u32[]{:S(2)}, u32[]{:S(2)}) %collective-permute-start.11) | collective-permute-done | bytes 589856 | tf_op jit(solution)/shard_map/ppermute | solution.py:19
  786.2 11.0 collective-permute-done.13
  839.5 87.1 %reduce-scatter.26.cloned.1.call-done = bf16[256,1152]{1,0:T(8,128)(2,1)} async-done(((bf16[2048,1152]{1,0:T(8,128)(2,1)}), bf16[256,1152]{1,0:T(8,128)(2,1)}) %reduce-scatter.26.cloned.1.call-update) | async-done | bytes 589840 | tf_op jit(solution)/shard_map/reduce_scatter | solution.py:299
  950.8 61.0 %all-gather.31.cloned.1.call-done = bf16[2048,1152]{1,0:T(8,128)(2,1)} async-done(((bf16[256,1152]{1,0:T(8,128)(2,1)}), bf16[2048,1152]{1,0:T(8,128)(2,1)}) %all-gather.31.cloned.1.call-update) | async-done | bytes 4718608 | tf_op jit(solution)/shard_map/all_gather | solution.py:313
  1025.9 22.7 %while.38 = (s32[]{:T(128)}, bf16[2,1024,2,72]{1,3,2,0:T(8,128)(2,1)}, bf16[2,1024,2,72]{1,3,2,0:T(8,128)(2,1)}, bf16[2,1024,2,72]{1,3,2,0:T(8,128)(2,1)}, bf16[...) while((s32[]{:T(128)}, ...), condition=%wide.region_24.25_spmd, body=%wide.region_22.24_spmd.sunk | while | flops 1535850496 | bytes 75363544 | solution.py:111
  1096.4 22.6 %reduce-scatter.38.cloned.1.call-done = bf16[288,144]{1,0:T(8,128)(2,1)} async-done(((bf16[1152,144]{1,0:T(8,128)(2,1)}), bf16[288,144]{1,0:T(8,128)(2,1)}) %reduce-scatter.38.cloned.1.call-update) | async-done | bytes 82960
  1120.8 22.8 %reduce-scatter.36.cloned.1.call-done = bf16[288,144]{1,0:T(8,128)(2,1)} async-done(((bf16[1152,144]{1,0:T(8,128)(2,1)}), bf16[288,144]{1,0:T(8,128)(2,1)}) %reduce-scatter.36.cloned.1.call-update) | async-done | bytes 82960
  1145.4 23.2 %reduce-scatter.34.cloned.1.call-done = bf16[288,144]{1,0:T(8,128)(2,1)} async-done(((bf16[1152,144]{1,0:T(8,128)(2,1)}), bf16[288,144]{1,0:T(8,128)(2,1)}) %reduce-scatter.34.cloned.1.call-update) | async-done | bytes 82960
  1170.3 97.1 %reduce-scatter.28.cloned.1.call-done = bf16[256,1152]{1,0:T(8,128)(2,1)} async-done(((bf16[2048,1152]{1,0:T(8,128)(2,1)}), bf16[256,1152]{1,0:T(8,128)(2,1)}) %reduce-scatter.28.cloned.1.call-update) | async-done | bytes 589840 | tf_op jit(solution)/shard_map/reduce_scatter | solution.py:331
  1269.4 36.3 %all-reduce.17 = (f32[1152]{0:T(1024)S(1)}, f32[1152]{0:T(1024)S(1)}, f32[1152]{0:T(1024)S(1)}, f32[1152]{0:T(1024)S(1)}, f32[1152]{0:T(1024)S(1)}, /*index=5*/f32[1152]{0:T(1024)S(1)}) all-reduce(f32[1152]{0:T(1024)S(1)} %get-tuple-element.226, f32[1152]{0:T(1024)S(1)} %get-tuple-element.231, ...), channel_id=7, replica_groups=mesh['gx'=4,'gy'=8] {'gy'}, use_global_device_ids=true, to_apply=%region_29.30.clone | all-reduce | flops 6912 | bytes 55296
  1306.2 10.7 all-reduce.18
  (406 shorter events, 409.9 us)
Async XLA Ops:
  8.1 86.1 %all-gather.17.cloned.1.call-start = ((), (), s32[]{:S(2)}) async-start(), calls=%async_computation.11 | async-start | bytes 5308416 | tf_op jit(solution)/shard_map/all_gather | solution.py:153
  8.8 223.0 %reduce-scatter.20.cloned.1.call-start = ((), (), s32[]{:S(2)}) async-start(), calls=%async_computation.12 | async-start | bytes 5308416 | tf_op jit(solution)/shard_map/reduce_scatter | solution.py:167
  138.2 200.3 %all-gather.19.cloned.1.call-start = ((), (), s32[]{:S(2)}) async-start(), calls=%async_computation.13 | async-start | bytes 1843200 | tf_op jit(solution)/shard_map/all_gather | solution.py:149
  138.8 199.8 %all-gather.21.cloned.1.call-start = ((), (), s32[]{:S(2)}) async-start(), calls=%async_computation.14 | async-start | bytes 1843200 | tf_op jit(solution)/shard_map/all_gather | solution.py:150
  236.8 27.7 %collective-permute-start.1 = (bf16[256,1152]{1,0:T(8,128)(2,1)S(1)}, bf16[256,1152]{1,0:T(8,128)(2,1)S(1)}, u32[]{:S(2)}, u32[]{:S(2)}) collective-permute-start(bf16[256,1152]{1,0:T(8,128)(2,1)S(1)} %get-tuple-element.303), channel_id=1, source_target_pairs={{0,7},{1,0},{2,1},{3,2},{4,3},{5,4},{6,5},{7,6},{8,15},{9,8},{10,9... | collective-permute-start | bytes 1769480 | tf_op jit(solution)/shard_map/ppermute | solution.py:24
  262.0 26.8 %collective-permute-start.2 = (bf16[256,1152]{1,0:T(8,128)(2,1)S(1)}, bf16[256,1152]{1,0:T(8,128)(2,1)S(1)}, u32[]{:S(2)}, u32[]{:S(2)}) collective-permute-start(bf16[256,1152]{1,0:T(8,128)(2,1)S(1)} %collective-permute-done), channel_id=1, source_target_pairs={{0,1},{1,2},{2,3},{3,4},{4,5},{5,6},{6,7},{7,0},{8,9},{9,10},{10,1... | collective-permute-start | bytes 1769480 | tf_op jit(solution)/shard_map/ppermute | solution.py:19
  264.5 28.6 %collective-permute-start.3 = (bf16[256,1152]{1,0:T(8,128)(2,1)S(1)}, bf16[256,1152]{1,0:T(8,128)(2,1)S(1)}, u32[]{:S(2)}, u32[]{:S(2)}) collective-permute-start(bf16[256,1152]{1,0:T(8,128)(2,1)S(1)} %collective-permute-done.1), channel_id=1, source_target_pairs={{0,7},{1,0},{2,1},{3,2},{4,3},{5,4},{6,5},{7,6},{8,15},{9,8},{10,9... | collective-permute-start | bytes 1769480 | tf_op jit(solution)/shard_map/ppermute | solution.py:24
  266.7 180.1 %reduce-scatter.22.cloned.1.call-start = ((), (), s32[]{:S(2)}) async-start(), calls=%async_computation.15 | async-start | bytes 5308416 | tf_op jit(solution)/shard_map/reduce_scatter | solution.py:184
  351.7 177.7 %all-gather.23.cloned.1.call-start = ((), (), s32[]{:S(2)}) async-start(), calls=%async_computation.16 | async-start | bytes 5308416 | tf_op jit(solution)/shard_map/all_gather | solution.py:153
  449.0 249.5 %reduce-scatter.24.cloned.1.call-start = ((), (), s32[]{:S(2)}) async-start(), calls=%async_computation.17 | async-start | bytes 5308416 | tf_op jit(solution)/shard_map/reduce_scatter | solution.py:167
  567.9 237.1 %all-gather.29.cloned.1.call-start = ((), (), s32[]{:S(2)}) async-start(), calls=%async_computation.20 | async-start | bytes 1843200 | tf_op jit(solution)/shard_map/all_gather | solution.py:149
  568.5 245.0 %all-gather.27.cloned.1.call-start = ((), (), s32[]{:S(2)}) async-start(), calls=%async_computation.19 | async-start | bytes 5308416 | tf_op jit(solution)/shard_map/all_gather | solution.py:281
  569.2 244.2 %all-gather.25.cloned.1.call-start = ((), (), s32[]{:S(2)}) async-start(), calls=%async_computation.18 | async-start | bytes 1843200 | tf_op jit(solution)/shard_map/all_gather | solution.py:150
  703.5 27.4 %collective-permute-start.8 = (bf16[256,1152]{1,0:T(8,128)(2,1)S(1)}, bf16[256,1152]{1,0:T(8,128)(2,1)}, u32[]{:S(2)}, u32[]{:S(2)}) collective-permute-start(bf16[256,1152]{1,0:T(8,128)(2,1)S(1)} %get-tuple-element.301), channel_id=1, source_target_pairs={{0,7},{1,0},{2,1},{3,2},{4,3},{5,4},{6,5},{7,6},{8,15},{9,8},{10,9... | collective-permute-start | bytes 1769480 | tf_op jit(solution)/shard_map/ppermute | solution.py:24
  731.0 29.3 %collective-permute-start.10 = (bf16[256,1152]{1,0:T(8,128)(2,1)}, bf16[256,1152]{1,0:T(8,128)(2,1)S(1)}, u32[]{:S(2)}, u32[]{:S(2)}) collective-permute-start(bf16[256,1152]{1,0:T(8,128)(2,1)} %collective-permute-done.8), channel_id=1, source_target_pairs={{0,7},{1,0},{2,1},{3,2},{4,3},{5,4},{6,5},{7,6},{8,15},{9,8},{10,9... | collective-permute-start | bytes 1769480 | tf_op jit(solution)/shard_map/ppermute | solution.py:24
  737.1 189.6 %reduce-scatter.26.cloned.1.call-start = ((), (), s32[]{:S(2)}) async-start(), calls=%async_computation.21 | async-start | bytes 5308416 | tf_op jit(solution)/shard_map/reduce_scatter | solution.py:299
  832.8 178.9 %all-gather.31.cloned.1.call-start = ((), (), s32[]{:S(2)}) async-start(), calls=%async_computation.22 | async-start | bytes 5308416 | tf_op jit(solution)/shard_map/all_gather | solution.py:313
  932.6 151.9 %reduce-scatter.32.cloned.1.call-start = ((), (), s32[]{:S(2)}) async-start(), calls=%async_computation.25 | async-start | bytes 1843200 | tf_op jit(solution)/shard_map/reduce_scatter | solution.py:292
  941.8 144.6 %reduce-scatter.30.cloned.1.call-start = ((), (), s32[]{:S(2)}) async-start(), calls=%async_computation.24 | async-start | bytes 1843200 | tf_op jit(solution)/shard_map/reduce_scatter | solution.py:286
  950.7 144.0 %reduce-scatter.40.cloned.1.call-start = ((), (), s32[]{:S(2)}) async-start(), calls=%async_computation.29 | async-start | bytes 737280
  1022.9 96.1 %reduce-scatter.38.cloned.1.call-start = ((), (), s32[]{:S(2)}) async-start(), calls=%async_computation.28 | async-start | bytes 737280
  1055.1 88.6 %reduce-scatter.36.cloned.1.call-start = ((), (), s32[]{:S(2)}) async-start(), calls=%async_computation.27 | async-start | bytes 737280
  1061.1 107.5 %reduce-scatter.34.cloned.1.call-start = ((), (), s32[]{:S(2)}) async-start(), calls=%async_computation.26 | async-start | bytes 737280
  1073.6 193.8 %reduce-scatter.28.cloned.1.call-start = ((), (), s32[]{:S(2)}) async-start(), calls=%async_computation.23 | async-start | bytes 5308416 | tf_op jit(solution)/shard_map/reduce_scatter | solution.py:331
  (71 other events, 3791.4 us)
Sparse Core Ops, SparseCore 0:
  11.1 83.0 all-gather.16
  138.3 93.3 reduce-scatter.19
  351.7 95.0 reduce-scatter.21
  449.1 80.1 all-gather.22
  568.0 130.4 reduce-scatter.23
Sparse Core Ops, SparseCore 1:
  140.2 17.1 all-gather.18
  266.8 17.2 all-gather.20
  569.9 17.1 all-gather.28
  589.3 101.6 all-gather.26
  737.1 17.4 all-gather.24
  832.9 93.6 reduce-scatter.25
  932.6 79.1 all-gather.30
  1014.2 25.8 reduce-scatter.31
  1042.6 27.4 reduce-scatter.29
  1072.7 22.0 reduce-scatter.39
  1097.1 22.0 reduce-scatter.37
  1121.6 22.0 reduce-scatter.35
  1146.6 22.0 reduce-scatter.33
  1172.2 95.2 reduce-scatter.27
